TPU v7x, 32 devices: a whole 2x2x4 slice. The times are simulated.
32 devices in a mesh: groups: 2 (over x), wide: 8 (over z, y), narrow: 2 (over core).
Axes of the slice: x: 2, y: 2, z: 4, core: 2. Of those that a mesh axis runs over, the one named last changes fastest.
Arguments:
- features: bfloat16 [64, 16, 128, 256], P(('groups', 'wide'), 'narrow'), parts along dimension 0, may hold values from -6 to 6
- tile_ids: int32 [64, 16, 3], P(('groups', 'wide'), 'narrow'), parts along dimension 0, may hold values from 0 to 15
- tiles: bfloat16 [16, 128, 128], replicated, may hold values from -0.25 to 0.25
- w_first: bfloat16 [256, 256], replicated, may hold values from -0.375 to 0.375
- w_second: bfloat16 [256, 256], replicated, may hold values from -0.375 to 0.375
- readout: bfloat16 [256], replicated, may hold values from -0.375 to 0.375
- target: float32 [64, 16, 128], P(('groups', 'wide'), 'narrow'), parts along dimension 0, may hold values from -6 to 6
Outputs:
- pred: float32 [64, 16, 128], P(('groups', 'wide'), 'narrow'), parts along dimension 0
- grad_first: float32 [512, 256], P(('groups', 'wide', 'narrow')), parts along dimension 0
- grad_second: float32 [512, 256], P(('groups', 'wide', 'narrow')), parts along dimension 0
- grad_readout: float32 [512], P('groups'), parts along dimension 0
There are 2 independent parts, one for each index of `groups`. A program takes and returns all parts, laid end to end along the dimension named above; an argument that names none is the same for every part. Nothing has to cross between parts.
All inputs are finite; a program needn't handle non-finite values.
Results may differ from a plain program's by a relative error of at most 0.0049.
Values may be sent and summed in bfloat16 or wider, within the bound.
No kernel may reach another device: no remote copies, remote signals or barrier semaphores. Data moves between devices by JAX's collectives and lax.ppermute only.
A program may use at most 128 MiB of HBM per device.

v0:
```python
import jax
import jax.numpy as jnp
from jax import lax
from jax.sharding import PartitionSpec as P


def extended(cells, sides, width):
    for axis, dim in sides:
        count = lax.axis_size(axis)
        ends = count - 1
        head = lax.slice_in_dim(cells, 0, width, axis=dim)
        tail = lax.slice_in_dim(cells, cells.shape[dim] - width, cells.shape[dim], axis=dim)
        cells = jnp.concatenate(
            [
                lax.ppermute(tail, axis, [(i, (i + 1) % count) for i in range(ends)]),
                cells,
                lax.ppermute(head, axis, [((i + 1) % count, i) for i in range(ends)]),
            ],
            axis=dim,
        )
    return cells


def shifted(block, axis, distance):
    devices = range(lax.axis_size(axis))
    route = [(i - distance, i) for i in devices if i - distance in devices]
    return lax.ppermute(block, axis, route)


def apply_operator(padded, ids_pad, tiles, offset):
    nx = padded.shape[0] - 2
    ny = padded.shape[1] - 2
    centre_ids = ids_pad[offset + 1 : offset + 1 + nx, offset + 1 : offset + 1 + ny]
    west_ids = ids_pad[offset : offset + nx, offset + 1 : offset + 1 + ny, 1]
    south_ids = ids_pad[offset + 1 : offset + 1 + nx, offset : offset + ny, 2]
    centre = padded[1:-1, 1:-1]
    selfs = jnp.take(tiles, centre_ids[..., 0], axis=0)
    total = jnp.einsum("xynm,xymh->xynh", selfs, centre, preferred_element_type=jnp.float32)
    total = total + jnp.einsum("xymn,xymh->xynh", selfs, centre, preferred_element_type=jnp.float32)
    east = jnp.take(tiles, centre_ids[..., 1], axis=0)
    total = total + jnp.einsum(
        "xynm,xymh->xynh", east, padded[2:, 1:-1], preferred_element_type=jnp.float32
    )
    west = jnp.take(tiles, west_ids, axis=0)
    total = total + jnp.einsum(
        "xymn,xymh->xynh", west, padded[:-2, 1:-1], preferred_element_type=jnp.float32
    )
    north = jnp.take(tiles, centre_ids[..., 2], axis=0)
    total = total + jnp.einsum(
        "xynm,xymh->xynh", north, padded[1:-1, 2:], preferred_element_type=jnp.float32
    )
    south = jnp.take(tiles, south_ids, axis=0)
    total = total + jnp.einsum(
        "xymn,xymh->xynh", south, padded[1:-1, :-2], preferred_element_type=jnp.float32
    )
    return total


def edge_rim(field):
    return extended(field, (("wide", 0), ("narrow", 1)), 1)


def column_term(matrix, grads):
    return lax.dot_general(
        matrix, grads, (((0,), (0,)), ((), ())), preferred_element_type=jnp.float32
    )


def per_device(features, tile_ids, tiles, w_first, w_second, readout, target):
    bx = features.shape[0]
    by = features.shape[1]
    width = features.shape[3]
    west_rim = shifted(tile_ids[bx - 1, :, 1], "wide", 1)
    south_rim = shifted(tile_ids[:, by - 1, 2], "narrow", 1)
    ids_pad = jnp.zeros((bx + 2, by + 2, 3), jnp.int32)
    ids_pad = ids_pad.at[1 : 1 + bx, 1 : 1 + by].set(tile_ids)
    ids_pad = ids_pad.at[0, 1 : 1 + by, 1].set(west_rim)
    ids_pad = ids_pad.at[1 : 1 + bx, 0, 2].set(south_rim)
    id_off = 0
    m_one = apply_operator(edge_rim(features), ids_pad, tiles, id_off).astype(jnp.bfloat16)
    z_one = jnp.einsum("xynh,hk->xynk", m_one, w_first, preferred_element_type=jnp.float32)
    x_one = (features.astype(jnp.float32) + jnp.tanh(z_one)).astype(jnp.bfloat16)
    m_two = apply_operator(edge_rim(x_one), ids_pad, tiles, id_off).astype(jnp.bfloat16)
    z_two = jnp.einsum("xynh,hk->xynk", m_two, w_second, preferred_element_type=jnp.float32)
    x_two = (x_one.astype(jnp.float32) + jnp.tanh(z_two)).astype(jnp.bfloat16)
    readf = readout.astype(jnp.float32)
    pred = jnp.einsum("xynh,h->xyn", x_two, readout, preferred_element_type=jnp.float32)
    nodes = bx * by * features.shape[2] * lax.axis_size("wide") * lax.axis_size("narrow")
    scale = jnp.sqrt(jnp.float32(width) / jnp.float32(nodes))
    grad_pred = (pred - target) * scale
    local_readout = jnp.einsum("xynh,xyn->h", x_two.astype(jnp.float32), grad_pred)
    grad_readout = lax.psum(local_readout, ("wide", "narrow"))
    grad_x_two = grad_pred[..., None] * readf
    tanh_two = jnp.tanh(z_two)
    grad_z_two = (grad_x_two * (1.0 - tanh_two * tanh_two)).astype(jnp.bfloat16)
    m_two_flat = m_two.reshape(-1, width)
    m_one_flat = m_one.reshape(-1, width)
    gz_two_flat = grad_z_two.reshape(-1, width)
    grad_second = lax.psum_scatter(
        column_term(m_two_flat, gz_two_flat), ("wide", "narrow"), scatter_dimension=0, tiled=True
    )
    grad_m_two = jnp.einsum(
        "xynk,hk->xynh", grad_z_two, w_second, preferred_element_type=jnp.float32
    ).astype(jnp.bfloat16)
    grad_pad = extended(grad_m_two, (("wide", 0), ("narrow", 1)), 1)
    grad_x_one = grad_x_two + apply_operator(grad_pad, ids_pad, tiles, id_off)
    tanh_one = jnp.tanh(z_one)
    grad_z_one = (grad_x_one * (1.0 - tanh_one * tanh_one)).astype(jnp.bfloat16)
    gz_one_flat = grad_z_one.reshape(-1, width)
    grad_first = lax.psum_scatter(
        column_term(m_one_flat, gz_one_flat), ("wide", "narrow"), scatter_dimension=0, tiled=True
    )
    return (pred, grad_first, grad_second, grad_readout)


def solution(mesh):
    in_specs = (
        P(("groups", "wide"), "narrow", None, None),
        P(("groups", "wide"), "narrow", None),
        P(),
        P(),
        P(),
        P(),
        P(("groups", "wide"), "narrow", None),
    )
    out_specs = (
        P(("groups", "wide"), "narrow", None),
        P(("groups", "wide", "narrow"), None),
        P(("groups", "wide", "narrow"), None),
        P("groups"),
    )
    return jax.shard_map(
        per_device, mesh=mesh, in_specs=in_specs, out_specs=out_specs, check_vma=False
    )
```

profile of v0, /device:TPU:0, one launch (start us, length us, event | category | flops | bytes accessed | tf_op | source)
XLA Modules:
  0.0 255.8 jit_solution(11594053089742596315)
XLA Ops:
  8.0 4.9 %collective-permute-start = (s32[8]{0:T(128)S(1)}, s32[8]{0:T(128)S(1)}, u32[]{:S(2)}, u32[]{:S(2)}) collective-permute-start(s32[8]{0:T(128)S(1)} %slice_bitcast_fusion.5), channel_id=1, source_target_pairs={{0,2},{2,4},{4,6},{6,8},{8,10},{10,12},{12,14},{1,3},{3,5},{5,7},{... | collective-permute-start | bytes 104 | tf_op jit(solution)/shard_map/ppermute | solution.py:27
  13.7 1.5 collective-permute-start.1
  15.2 2.3 fusion.94
  17.5 3.4 %collective-permute-start.3 = (bf16[1,8,128,256]{3,2,1,0:T(8,128)(2,1)}, bf16[1,8,128,256]{3,2,1,0:T(8,128)(2,1)S(1)}, u32[]{:S(2)}, u32[]{:S(2)}) collective-permute-start(bf16[1,8,128,256]{3,2,1,0:T(8,128)(2,1)} %get-tuple-element.52), channel_id=1, source_target_pairs={{0,2},{2,4},{4,6},{6,8},{8,10},{10,12},{12,14},{1,3},{3,5},{5,7},{... | collective-permute-start | bytes 1572872 | tf_op jit(solution)/shard_map/ppermute | solution.py:15
  20.9 1.3 collective-permute-start.2
  24.8 1.7 gather_fusion
  26.5 2.2 copy.13
  28.8 4.0 %fusion.46 = f32[4,8,128,256]{3,2,1,0:T(8,128)} fusion(bf16[4,8,128,256]{3,2,1,0:T(8,128)(2,1)S(1)} %copy-done.2, bf16[4,8,128,128]{2,3,1,0:T(8,128)(2,1)} %copy.13, pred[4,8]{1,0:T(4,128)(4,1)S(1)} %get-tuple-element.57), kind=kOutput, calls=%fused_computation.83 | convolution fusion | flops 268959744 | bytes 7340064 | tf_op jit(solution)/shard_map/xymn,xymh->xynh/dot_general | solution.py:39
  32.7 1.6 gather_fusion.3
  34.5 1.7 gather_fusion.2
  36.2 2.3 copy.15
  38.5 1.7 gather_fusion.1
  40.2 1.7 gather_fusion.4
  41.8 2.3 copy.16
  44.1 4.4 %fusion.47 = f32[4,8,128,256]{3,2,1,0:T(8,128)} fusion(bf16[4,8,128,256]{3,2,1,0:T(8,128)(2,1)S(1)} %copy-done.2, bf16[4,8,128,128]{2,3,1,0:T(8,128)(2,1)} %copy.13, pred[4,8]{1,0:T(4,128)(4,1)S(1)} %get-tuple-element.57), kind=kOutput, calls=%fused_computation.84 | convolution fusion | flops 268959744 | bytes 7340064 | tf_op jit(solution)/shard_map/xynm,xymh->xynh/dot_general | solution.py:38
  49.9 1.3 collective-permute-start.4
  51.2 3.1 %collective-permute-start.5 = (bf16[6,1,128,256]{3,2,1,0:T(8,128)(2,1)S(1)}, bf16[6,1,128,256]{3,2,1,0:T(8,128)(2,1)S(1)}, u32[]{:S(2)}, u32[]{:S(2)}) collective-permute-start(bf16[6,1,128,256]{3,2,1,0:T(8,128)(2,1)S(1)} %get-tuple-element.45), channel_id=1, source_target_pairs={{0,1},{2,3},{4,5},{6,7},{8,9},{10,11},{12,13},{14,15},{16,17},{18,... | collective-permute-start | bytes 1179656 | tf_op jit(solution)/shard_map/ppermute | solution.py:15
  55.6 1.9 fusion.25
  57.5 2.9 %fusion.21 = f32[4,8,128,256]{3,2,1,0:T(8,128)} fusion(bf16[6,1,128,256]{3,2,1,0:T(8,128)(2,1)S(1)} %collective-permute-done.4, bf16[6,8,128,256]{3,2,1,0:T(8,128)(2,1)S(1)} %constant_dynamic-update-slice_fusion, bf16[4,8,128,128]{3,2,1,0:T(8,128)(2,1)S(1)} %bitcast.88, pred[4,8]{1,0:T(4,128)(4,1)S(1)} %get-tuple-element.54), kind=kOutput, calls=%fused_computation.50 | convolution fusion | flops 270008320 | bytes 8781856 | tf_op jit(solution)/shard_map/xynm,xymh->xynh/dot_general | solution.py:49
  61.5 7.3 %add_convert_fusion.3 = bf16[4,8,128,256]{3,2,1,0:T(8,128)(2,1)} fusion(f32[4,8,128,256]{3,2,1,0:T(8,128)} %fusion.21, f32[4,8,128,256]{3,2,1,0:T(8,128)S(1)} %fusion.23, f32[4,8,128,256]{3,2,1,0:T(8,128)S(1)} %fusion.25, f32[4,8,128,256]{3,2,1,0:T(8,128)} %fusion.47, f32[4,8,128,256]{3,2,1,0:T(8,128)S(1)} %copy-done.13, ...), kind=kOutput, calls=%fused_computation.13 | convolution fusion | flops 276299776 | bytes 27656224 | tf_op jit(solution)/shard_map/xymn,xymh->xynh/dot_general | solution.py:53
  68.8 4.4 %add_convert_fusion.2 = (bf16[4,8,128,256]{3,2,1,0:T(8,128)(2,1)S(1)}, f32[4,8,128,256]{3,2,1,0:T(8,128)}) fusion(bf16[4,8,128,256]{3,2,1,0:T(8,128)(2,1)S(1)} %copy-done.3, bf16[4,8,128,256]{3,2,1,0:T(8,128)(2,1)} %add_convert_fusion.3, bf16[256,256]{1,0:T(8,128)(2,1)S(1)} %copy-done.19), kind=kOutput, calls=%fused_computation.12 | convolution fusion | flops 540016640 | bytes 10616832 | tf_op jit(solution)/shard_map/xynh,hk->xynk/dot_general | solution.py:81
  73.2 1.4 collective-permute-start.6
  74.7 5.2 %collective-permute-start.7 = (bf16[1,8,128,256]{3,2,1,0:T(8,128)(2,1)S(1)}, bf16[1,8,128,256]{3,2,1,0:T(8,128)(2,1)S(1)}, u32[]{:S(2)}, u32[]{:S(2)}) collective-permute-start(bf16[1,8,128,256]{3,2,1,0:T(8,128)(2,1)S(1)} %get-tuple-element.49), channel_id=1, source_target_pairs={{0,2},{2,4},{4,6},{6,8},{8,10},{10,12},{12,14},{1,3},{3,5},{5,7},{... | collective-permute-start | bytes 1572872 | tf_op jit(solution)/shard_map/ppermute | solution.py:15
  80.7 3.2 %fusion.45 = f32[4,8,128,256]{3,2,1,0:T(8,128)} fusion(bf16[4,8,128,256]{3,2,1,0:T(8,128)(2,1)S(1)} %get-tuple-element.63, bf16[4,8,128,128]{2,3,1,0:T(8,128)(2,1)S(1)} %copy-done.6, pred[4,8]{1,0:T(4,128)(4,1)S(1)} %get-tuple-element.57), kind=kOutput, calls=%fused_computation.82 | convolution fusion | flops 268959744 | bytes 7340064 | tf_op jit(solution)/shard_map/xynm,xymh->xynh/dot_general | solution.py:38
  83.9 5.4 %collective-permute-done.6 = bf16[1,8,128,256]{3,2,1,0:T(8,128)(2,1)S(1)} collective-permute-done((bf16[1,8,128,256]{3,2,1,0:T(8,128)(2,1)S(1)}, bf16[1,8,128,256]{3,2,1,0:T(8,128)(2,1)S(1)}, u32[]{:S(2)}, u32[]{:S(2)}) %collective-permute-start.6) | collective-permute-done | bytes 524320 | tf_op jit(solution)/shard_map/ppermute | solution.py:17
  89.4 11.4 %collective-permute-done.7 = bf16[1,8,128,256]{3,2,1,0:T(8,128)(2,1)S(1)} collective-permute-done((bf16[1,8,128,256]{3,2,1,0:T(8,128)(2,1)S(1)}, bf16[1,8,128,256]{3,2,1,0:T(8,128)(2,1)S(1)}, u32[]{:S(2)}, u32[]{:S(2)}) %collective-permute-start.7) | collective-permute-done | bytes 524320 | tf_op jit(solution)/shard_map/ppermute | solution.py:15
  100.8 1.3 collective-permute-start.8
  102.1 3.3 %collective-permute-start.9 = (bf16[6,1,128,256]{3,2,1,0:T(8,128)(2,1)S(1)}, bf16[6,1,128,256]{3,2,1,0:T(8,128)(2,1)S(1)}, u32[]{:S(2)}, u32[]{:S(2)}) collective-permute-start(bf16[6,1,128,256]{3,2,1,0:T(8,128)(2,1)S(1)} %get-tuple-element.43), channel_id=1, source_target_pairs={{0,1},{2,3},{4,5},{6,7},{8,9},{10,11},{12,13},{14,15},{16,17},{18,... | collective-permute-start | bytes 1179656 | tf_op jit(solution)/shard_map/ppermute | solution.py:15
  107.4 2.8 %fusion.13 = f32[4,8,128,256]{3,2,1,0:T(8,128)} fusion(bf16[6,1,128,256]{3,2,1,0:T(8,128)(2,1)S(1)} %collective-permute-done.8, bf16[1,8,128,256]{3,2,1,0:T(8,128)(2,1)S(1)} %collective-permute-done.6, bf16[4,8,128,256]{3,2,1,0:T(8,128)(2,1)S(1)} %get-tuple-element.63, bf16[1,8,128,256]{3,2,1,0:T(8,128)(2,1)S(1)} %collective-permute-done.7, ...), kind=kOutput, calls=%fused_computation.36 | convolution fusion | flops 272105472 | bytes 8781856 | tf_op jit(solution)/shard_map/xynm,xymh->xynh/dot_general | solution.py:49
  110.2 4.7 %add_convert_fusion.1 = bf16[4,8,128,256]{3,2,1,0:T(8,128)(2,1)S(1)} fusion(f32[4,8,128,256]{3,2,1,0:T(8,128)} %fusion.13, f32[4,8,128,256]{3,2,1,0:T(8,128)S(1)} %fusion.15, f32[4,8,128,256]{3,2,1,0:T(8,128)S(1)} %fusion.17, f32[4,8,128,256]{3,2,1,0:T(8,128)} %fusion.45, f32[4,8,128,256]{3,2,1,0:T(8,128)S(1)} %fusion.44, ...), kind=kOutput, calls=%fused_computation.11 | convolution fusion | flops 278396928 | bytes 27656224 | tf_op jit(solution)/shard_map/xymn,xymh->xynh/dot_general | solution.py:53
  116.4 1.2 copy-done.8
  117.6 2.3 convolution_bitcast_fusion
  119.9 3.2 %convolution_convert_fusion = bf16[4,8,128,256]{3,2,1,0:T(8,128)(2,1)S(1)} fusion(bf16[256,256]{1,0:T(8,128)(2,1)S(1)} %copy-done.20, f32[4,8,128,256]{3,2,1,0:T(8,128)} %copy-done.8, f32[256]{0:T(256)S(1)} %copy-done.33, f32[4,8,128]{2,1,0:T(8,128)S(1)} %subtract_multiply_fusion), kind=kOutput, calls=%fused_computation.58 | convolution fusion | flops 543162368 | bytes 6439936 | tf_op jit(solution)/shard_map/xynk,hk->xynh/dot_general | solution.py:102
  124.2 1.4 collective-permute-start.10
  125.6 5.0 %collective-permute-start.11 = (bf16[1,8,128,256]{3,2,1,0:T(8,128)(2,1)}, bf16[1,8,128,256]{3,2,1,0:T(8,128)(2,1)S(1)}, u32[]{:S(2)}, u32[]{:S(2)}) collective-permute-start(bf16[1,8,128,256]{3,2,1,0:T(8,128)(2,1)} %get-tuple-element.47), channel_id=1, source_target_pairs={{0,2},{2,4},{4,6},{6,8},{8,10},{10,12},{12,14},{1,3},{3,5},{5,7},{... | collective-permute-start | bytes 1572872 | tf_op jit(solution)/shard_map/ppermute | solution.py:15
  130.7 2.7 %fusion.42 = f32[4,8,128,256]{3,2,1,0:T(8,128)} fusion(bf16[4,8,128,256]{3,2,1,0:T(8,128)(2,1)S(1)} %convolution_convert_fusion, bf16[4,8,128,128]{2,3,1,0:T(8,128)(2,1)S(1)} %copy-done.7, pred[4,8]{1,0:T(4,128)(4,1)S(1)} %copy-done.22), kind=kOutput, calls=%fused_computation.79 | convolution fusion | flops 268959744 | bytes 7340064 | tf_op jit(solution)/shard_map/xymn,xymh->xynh/dot_general | solution.py:39
  133.5 5.3 %fusion.43 = f32[4,8,128,256]{3,2,1,0:T(8,128)} fusion(bf16[4,8,128,256]{3,2,1,0:T(8,128)(2,1)} %copy-done.4, bf16[4,8,128,128]{2,3,1,0:T(8,128)(2,1)} %copy.13, pred[4,8]{1,0:T(4,128)(4,1)S(1)} %copy-done.22), kind=kOutput, calls=%fused_computation.80 | convolution fusion | flops 268959744 | bytes 7340064 | tf_op jit(solution)/shard_map/xynm,xymh->xynh/dot_general | solution.py:38
  138.7 1.6 collective-permute-done.10
  140.3 11.5 %collective-permute-done.11 = bf16[1,8,128,256]{3,2,1,0:T(8,128)(2,1)S(1)} collective-permute-done((bf16[1,8,128,256]{3,2,1,0:T(8,128)(2,1)}, bf16[1,8,128,256]{3,2,1,0:T(8,128)(2,1)S(1)}, u32[]{:S(2)}, u32[]{:S(2)}) %collective-permute-start.11) | collective-permute-done | bytes 524320 | tf_op jit(solution)/shard_map/ppermute | solution.py:15
  151.9 1.3 collective-permute-start.12
  153.2 3.4 %collective-permute-start.13 = (bf16[6,1,128,256]{3,2,1,0:T(8,128)(2,1)S(1)}, bf16[6,1,128,256]{3,2,1,0:T(8,128)(2,1)S(1)}, u32[]{:S(2)}, u32[]{:S(2)}) collective-permute-start(bf16[6,1,128,256]{3,2,1,0:T(8,128)(2,1)S(1)} %get-tuple-element.41), channel_id=1, source_target_pairs={{0,1},{2,3},{4,5},{6,7},{8,9},{10,11},{12,13},{14,15},{16,17},{18,... | collective-permute-start | bytes 1179656 | tf_op jit(solution)/shard_map/ppermute | solution.py:15
  156.7 2.8 %fusion.9 = f32[4,8,128,256]{3,2,1,0:T(8,128)} fusion(bf16[1,8,128,256]{3,2,1,0:T(8,128)(2,1)S(1)} %collective-permute-done.10, bf16[4,8,128,256]{3,2,1,0:T(8,128)(2,1)S(1)} %copy-done.5, bf16[4,8,128,128]{3,2,1,0:T(8,128)(2,1)S(1)} %bitcast.87, pred[4,8]{1,0:T(4,128)(4,1)S(1)} %copy-done.26), kind=kOutput, calls=%fused_computation.28 | convolution fusion | flops 270008320 | bytes 7864352 | tf_op jit(solution)/shard_map/xynm,xymh->xynh/dot_general | solution.py:41
  159.5 2.8 %fusion.7 = f32[4,8,128,256]{3,2,1,0:T(8,128)} fusion(bf16[4,8,128,256]{3,2,1,0:T(8,128)(2,1)S(1)} %copy-done.5, bf16[1,8,128,256]{3,2,1,0:T(8,128)(2,1)S(1)} %collective-permute-done.11, bf16[4,8,128,128]{2,3,1,0:T(8,128)(2,1)S(1)} %copy-done.10, pred[4,8]{1,0:T(4,128)(4,1)S(1)} %copy-done.24), kind=kOutput, calls=%fused_computation.25 | convolution fusion | flops 270008320 | bytes 7864352 | tf_op jit(solution)/shard_map/xymn,xymh->xynh/dot_general | solution.py:45
  162.3 2.9 %fusion.5 = f32[4,8,128,256]{3,2,1,0:T(8,128)} fusion(bf16[6,1,128,256]{3,2,1,0:T(8,128)(2,1)S(1)} %collective-permute-done.12, bf16[1,8,128,256]{3,2,1,0:T(8,128)(2,1)S(1)} %collective-permute-done.10, bf16[4,8,128,256]{3,2,1,0:T(8,128)(2,1)S(1)} %copy-done.5, bf16[1,8,128,256]{3,2,1,0:T(8,128)(2,1)S(1)} %collective-permute-done.11, ...), kind=kOutput, calls=%fused_computation.20 | convolution fusion | flops 272105472 | bytes 8781856 | tf_op jit(solution)/shard_map/xynm,xymh->xynh/dot_general | solution.py:49
  165.1 13.3 %fusion.28 = f32[256,256]{1,0:T(8,128)} fusion(bf16[4,8,128,256]{3,2,1,0:T(8,128)(2,1)} %add_convert_fusion.3, f32[4,8,128,256]{3,2,1,0:T(8,128)} %fusion.5, f32[4,8,128,256]{3,2,1,0:T(8,128)} %fusion.7, f32[4,8,128,256]{3,2,1,0:T(8,128)} %fusion.9, f32[4,8,128,256]{3,2,1,0:T(8,128)} %fusion.43, f32[4,8,128,256]{3,2,1,0:T(8,128)} %fusion.42, ...), kind=kOutput, calls=%fused_computation.60 | convolution fusion | flops 820510720 | bytes 32130080 | tf_op jit(solution)/shard_map/dot_general | solution.py:64
  178.5 2.9 %fusion.90 = f32[1,256,1,1]{1,0,3,2:T(1,128)S(1)} fusion(f32[4,8,128,1]{2,3,1,0:T(1,128)S(1)} %bitcast.94, bf16[4,8,128,256]{3,2,1,0:T(8,128)(2,1)S(1)} %get-tuple-element.63, f32[4,8,128,256]{3,2,1,0:T(8,128)} %copy-done.8), kind=kOutput, calls=%fused_computation.155 | convolution fusion | flops 5242880 | bytes 6308864 | tf_op jit(solution)/shard_map/xynh,xyn->h/dot_general | solution.py:91
  181.4 31.6 %psum.7 = f32[256]{0:T(256)} all-reduce(f32[256]{0:T(256)S(1)} %bitcast.97), channel_id=1, replica_groups=mesh['groups'=2,'wide'=8,'narrow'=2] {'wide','narrow'}, use_global_device_ids=true, to_apply=%region_2.4 | all-reduce | flops 256 | bytes 2048 | tf_op jit(solution)/shard_map/psum | solution.py:92
  213.0 35.9 %reduce-scatter.3.cloned.1.call-done = f32[16,256]{1,0:T(8,128)} async-done(((f32[256,256]{1,0:T(8,128)}), f32[16,256]{1,0:T(8,128)}) %reduce-scatter.3.cloned.1.call-update) | async-done | bytes 16400 | tf_op jit(solution)/shard_map/reduce_scatter | solution.py:110
  (119 shorter events, 13.8 us)
Async XLA Ops:
  7.2 17.6 %copy-start = (bf16[16,128,128]{2,1,0:T(8,128)(2,1)S(1)}, bf16[16,128,128]{2,1,0:T(8,128)(2,1)}, u32[]{:S(2)}) copy-start(bf16[16,128,128]{2,1,0:T(8,128)(2,1)} %param.17) | copy-start | bytes 1572868
  7.2 16.2 %copy-start.31 = (s32[4,8,3]{1,0,2:T(4,128)S(1)}, s32[4,8,3]{1,0,2:T(4,128)}, u32[]{:S(2)}) copy-start(s32[4,8,3]{1,0,2:T(4,128)} %param.16) | copy-start | bytes 1156
  7.2 15.0 %copy-start.35 = (bf16[256]{0:T(256)(128)(2,1)S(1)}, bf16[256]{0:T(256)(128)(2,1)}, u32[]{:S(2)}) copy-start(bf16[256]{0:T(256)(128)(2,1)} %param.20) | copy-start | bytes 1540
  7.2 205.8 %reduce-scatter.5.cloned.1.call-start = ((), (), s32[]{:S(2)}) async-start(), calls=%async_computation.3 | async-start | bytes 278528 | tf_op jit(solution)/shard_map/reduce_scatter | solution.py:99
  8.0 15.6 %collective-permute-start = (s32[8]{0:T(128)S(1)}, s32[8]{0:T(128)S(1)}, u32[]{:S(2)}, u32[]{:S(2)}) collective-permute-start(s32[8]{0:T(128)S(1)} %slice_bitcast_fusion.5), channel_id=1, source_target_pairs={{0,2},{2,4},{4,6},{6,8},{8,10},{10,12},{12,14},{1,3},{3,5},{5,7},{... | collective-permute-start | bytes 104 | tf_op jit(solution)/shard_map/ppermute | solution.py:27
  13.7 9.7 %collective-permute-start.1 = (s32[4]{0:T(128)S(1)}, s32[4]{0:T(128)S(1)}, u32[]{:S(2)}, u32[]{:S(2)}) collective-permute-start(s32[4]{0:T(128)S(1)} %slice_reduce_fusion), channel_id=1, source_target_pairs={{0,1},{2,3},{4,5},{6,7},{8,9},{10,11},{12,13},{14,15},{16,17},{18,... | collective-permute-start | bytes 56 | tf_op jit(solution)/shard_map/ppermute | solution.py:27
  17.5 31.0 %collective-permute-start.3 = (bf16[1,8,128,256]{3,2,1,0:T(8,128)(2,1)}, bf16[1,8,128,256]{3,2,1,0:T(8,128)(2,1)S(1)}, u32[]{:S(2)}, u32[]{:S(2)}) collective-permute-start(bf16[1,8,128,256]{3,2,1,0:T(8,128)(2,1)} %get-tuple-element.52), channel_id=1, source_target_pairs={{0,2},{2,4},{4,6},{6,8},{8,10},{10,12},{12,14},{1,3},{3,5},{5,7},{... | collective-permute-start | bytes 1572872 | tf_op jit(solution)/shard_map/ppermute | solution.py:15
  20.9 27.8 %collective-permute-start.2 = (bf16[1,8,128,256]{3,2,1,0:T(8,128)(2,1)}, bf16[1,8,128,256]{3,2,1,0:T(8,128)(2,1)}, u32[]{:S(2)}, u32[]{:S(2)}) collective-permute-start(bf16[1,8,128,256]{3,2,1,0:T(8,128)(2,1)} %get-tuple-element.51), channel_id=1, source_target_pairs={{2,0},{4,2},{6,4},{8,6},{10,8},{12,10},{14,12},{3,1},{5,3},{7,5},{... | collective-permute-start | bytes 1572872 | tf_op jit(solution)/shard_map/ppermute | solution.py:17
  24.5 56.1 %copy-start.21 = (pred[4,8]{1,0:T(4,128)(4,1)}, pred[4,8]{1,0:T(4,128)(4,1)S(1)}, u32[]{:S(2)}) copy-start(pred[4,8]{1,0:T(4,128)(4,1)S(1)} %get-tuple-element.57) | copy-start | bytes 100
  24.5 80.9 %copy-start.25 = (pred[4,8]{1,0:T(4,128)(4,1)}, pred[4,8]{1,0:T(4,128)(4,1)S(1)}, u32[]{:S(2)}) copy-start(pred[4,8]{1,0:T(4,128)(4,1)S(1)} %get-tuple-element.56) | copy-start | bytes 100
  24.5 81.7 %copy-start.23 = (pred[4,8]{1,0:T(4,128)(4,1)}, pred[4,8]{1,0:T(4,128)(4,1)S(1)}, u32[]{:S(2)}) copy-start(pred[4,8]{1,0:T(4,128)(4,1)S(1)} %get-tuple-element.55) | copy-start | bytes 100
  24.5 82.5 %copy-start.29 = (pred[4,8]{1,0:T(4,128)(4,1)}, pred[4,8]{1,0:T(4,128)(4,1)S(1)}, u32[]{:S(2)}) copy-start(pred[4,8]{1,0:T(4,128)(4,1)S(1)} %get-tuple-element.54) | copy-start | bytes 100
  24.8 3.9 %copy-start.2 = (bf16[4,8,128,256]{3,2,1,0:T(8,128)(2,1)S(1)}, bf16[4,8,128,256]{3,2,1,0:T(8,128)(2,1)}, u32[]{:S(2)}) copy-start(bf16[4,8,128,256]{3,2,1,0:T(8,128)(2,1)} %param.15) | copy-start | bytes 6291460
  48.7 5.6 %copy-start.9 = (bf16[4,8,128,128]{2,3,1,0:T(8,128)(2,1)S(1)}, bf16[4,8,128,128]{2,3,1,0:T(8,128)(2,1)}, u32[]{:S(2)}) copy-start(bf16[4,8,128,128]{2,3,1,0:T(8,128)(2,1)} %copy.15) | copy-start | bytes 3145732
  49.9 7.6 %copy-start.14 = (bf16[6,8,128,256]{3,2,1,0:T(8,128)(2,1)}, bf16[6,8,128,256]{3,2,1,0:T(8,128)(2,1)S(1)}, u32[]{:S(2)}) copy-start(bf16[6,8,128,256]{3,2,1,0:T(8,128)(2,1)S(1)} %constant_dynamic-update-slice_fusion) | copy-start | bytes 9437188
  49.9 7.5 %collective-permute-start.4 = (bf16[6,1,128,256]{3,2,1,0:T(8,128)(2,1)S(1)}, bf16[6,1,128,256]{3,2,1,0:T(8,128)(2,1)S(1)}, u32[]{:S(2)}, u32[]{:S(2)}) collective-permute-start(bf16[6,1,128,256]{3,2,1,0:T(8,128)(2,1)S(1)} %get-tuple-element.46), channel_id=1, source_target_pairs={{1,0},{3,2},{5,4},{7,6},{9,8},{11,10},{13,12},{15,14},{17,16},{19,... | collective-permute-start | bytes 1179656 | tf_op jit(solution)/shard_map/ppermute | solution.py:17
  51.2 9.2 %collective-permute-start.5 = (bf16[6,1,128,256]{3,2,1,0:T(8,128)(2,1)S(1)}, bf16[6,1,128,256]{3,2,1,0:T(8,128)(2,1)S(1)}, u32[]{:S(2)}, u32[]{:S(2)}) collective-permute-start(bf16[6,1,128,256]{3,2,1,0:T(8,128)(2,1)S(1)} %get-tuple-element.45), channel_id=1, source_target_pairs={{0,1},{2,3},{4,5},{6,7},{8,9},{10,11},{12,13},{14,15},{16,17},{18,... | collective-permute-start | bytes 1179656 | tf_op jit(solution)/shard_map/ppermute | solution.py:15
  55.5 1.9 copy-start.16
  57.5 3.3 %copy-start.13 = (f32[4,8,128,256]{3,2,1,0:T(8,128)S(1)}, f32[4,8,128,256]{3,2,1,0:T(8,128)}, u32[]{:S(2)}) copy-start(f32[4,8,128,256]{3,2,1,0:T(8,128)} %fusion.46) | copy-start | bytes 12582916
  57.5 4.0 %copy-start.15 = (bf16[4,8,128,128]{2,3,1,0:T(8,128)(2,1)S(1)}, bf16[4,8,128,128]{2,3,1,0:T(8,128)(2,1)}, u32[]{:S(2)}) copy-start(bf16[4,8,128,128]{2,3,1,0:T(8,128)(2,1)} %copy.16) | copy-start | bytes 3145732
  57.5 4.0 %copy-start.32 = (pred[4,8]{1,0:T(4,128)(4,1)S(1)}, pred[4,8]{1,0:T(4,128)(4,1)}, u32[]{:S(2)}) copy-start(pred[4,8]{1,0:T(4,128)(4,1)} %get-tuple-element.53) | copy-start | bytes 100
  61.5 7.3 %copy-start.3 = (bf16[4,8,128,256]{3,2,1,0:T(8,128)(2,1)S(1)}, bf16[4,8,128,256]{3,2,1,0:T(8,128)(2,1)}, u32[]{:S(2)}) copy-start(bf16[4,8,128,256]{3,2,1,0:T(8,128)(2,1)} %param.15) | copy-start | bytes 6291460
  61.5 7.3 %copy-start.19 = (bf16[256,256]{1,0:T(8,128)(2,1)S(1)}, bf16[256,256]{1,0:T(8,128)(2,1)}, u32[]{:S(2)}) copy-start(bf16[256,256]{1,0:T(8,128)(2,1)} %param.18) | copy-start | bytes 393220
  73.1 6.7 %copy-start.6 = (bf16[4,8,128,128]{2,3,1,0:T(8,128)(2,1)S(1)}, bf16[4,8,128,128]{2,3,1,0:T(8,128)(2,1)}, u32[]{:S(2)}) copy-start(bf16[4,8,128,128]{2,3,1,0:T(8,128)(2,1)} %copy.13) | copy-start | bytes 3145732
  73.2 16.1 %collective-permute-start.6 = (bf16[1,8,128,256]{3,2,1,0:T(8,128)(2,1)S(1)}, bf16[1,8,128,256]{3,2,1,0:T(8,128)(2,1)S(1)}, u32[]{:S(2)}, u32[]{:S(2)}) collective-permute-start(bf16[1,8,128,256]{3,2,1,0:T(8,128)(2,1)S(1)} %get-tuple-element.50), channel_id=1, source_target_pairs={{2,0},{4,2},{6,4},{8,6},{10,8},{12,10},{14,12},{3,1},{5,3},{7,5},{... | collective-permute-start | bytes 1572872 | tf_op jit(solution)/shard_map/ppermute | solution.py:17
  74.7 26.1 %collective-permute-start.7 = (bf16[1,8,128,256]{3,2,1,0:T(8,128)(2,1)S(1)}, bf16[1,8,128,256]{3,2,1,0:T(8,128)(2,1)S(1)}, u32[]{:S(2)}, u32[]{:S(2)}) collective-permute-start(bf16[1,8,128,256]{3,2,1,0:T(8,128)(2,1)S(1)} %get-tuple-element.49), channel_id=1, source_target_pairs={{0,2},{2,4},{4,6},{6,8},{8,10},{10,12},{12,14},{1,3},{3,5},{5,7},{... | collective-permute-start | bytes 1572872 | tf_op jit(solution)/shard_map/ppermute | solution.py:15
  100.8 6.2 %collective-permute-start.8 = (bf16[6,1,128,256]{3,2,1,0:T(8,128)(2,1)S(1)}, bf16[6,1,128,256]{3,2,1,0:T(8,128)(2,1)S(1)}, u32[]{:S(2)}, u32[]{:S(2)}) collective-permute-start(bf16[6,1,128,256]{3,2,1,0:T(8,128)(2,1)S(1)} %get-tuple-element.44), channel_id=1, source_target_pairs={{1,0},{3,2},{5,4},{7,6},{9,8},{11,10},{13,12},{15,14},{17,16},{19,... | collective-permute-start | bytes 1179656 | tf_op jit(solution)/shard_map/ppermute | solution.py:17
  102.1 8.1 %collective-permute-start.9 = (bf16[6,1,128,256]{3,2,1,0:T(8,128)(2,1)S(1)}, bf16[6,1,128,256]{3,2,1,0:T(8,128)(2,1)S(1)}, u32[]{:S(2)}, u32[]{:S(2)}) collective-permute-start(bf16[6,1,128,256]{3,2,1,0:T(8,128)(2,1)S(1)} %get-tuple-element.43), channel_id=1, source_target_pairs={{0,1},{2,3},{4,5},{6,7},{8,9},{10,11},{12,13},{14,15},{16,17},{18,... | collective-permute-start | bytes 1179656 | tf_op jit(solution)/shard_map/ppermute | solution.py:15
  110.2 4.7 %copy-start.20 = (bf16[256,256]{1,0:T(8,128)(2,1)S(1)}, bf16[256,256]{1,0:T(8,128)(2,1)}, u32[]{:S(2)}) copy-start(bf16[256,256]{1,0:T(8,128)(2,1)} %param.19) | copy-start | bytes 393220
  115.6 2.0 copy-start.8
  115.6 2.0 copy-start.33
  116.4 3.5 %copy-start.27 = (f32[1,4,8,128]{3,0,2,1:T(1,128)}, f32[1,4,8,128]{3,0,2,1:T(1,128)S(1)}, u32[]{:S(2)}) copy-start(f32[1,4,8,128]{3,0,2,1:T(1,128)S(1)} %fusion.53) | copy-start | bytes 49156
  123.1 7.6 %copy-start.4 = (bf16[4,8,128,256]{3,2,1,0:T(8,128)(2,1)}, bf16[4,8,128,256]{3,2,1,0:T(8,128)(2,1)S(1)}, u32[]{:S(2)}) copy-start(bf16[4,8,128,256]{3,2,1,0:T(8,128)(2,1)S(1)} %convolution_convert_fusion) | copy-start | bytes 6291460
  123.1 7.6 %copy-start.7 = (bf16[4,8,128,128]{2,3,1,0:T(8,128)(2,1)S(1)}, bf16[4,8,128,128]{2,3,1,0:T(8,128)(2,1)}, u32[]{:S(2)}) copy-start(bf16[4,8,128,128]{2,3,1,0:T(8,128)(2,1)} %copy.13) | copy-start | bytes 3145732
  123.1 7.6 %copy-start.22 = (pred[4,8]{1,0:T(4,128)(4,1)S(1)}, pred[4,8]{1,0:T(4,128)(4,1)}, u32[]{:S(2)}) copy-start(pred[4,8]{1,0:T(4,128)(4,1)} %copy-done.21) | copy-start | bytes 100
  124.2 16.2 %collective-permute-start.10 = (bf16[1,8,128,256]{3,2,1,0:T(8,128)(2,1)}, bf16[1,8,128,256]{3,2,1,0:T(8,128)(2,1)S(1)}, u32[]{:S(2)}, u32[]{:S(2)}) collective-permute-start(bf16[1,8,128,256]{3,2,1,0:T(8,128)(2,1)} %get-tuple-element.48), channel_id=1, source_target_pairs={{2,0},{4,2},{6,4},{8,6},{10,8},{12,10},{14,12},{3,1},{5,3},{7,5},{... | collective-permute-start | bytes 1572872 | tf_op jit(solution)/shard_map/ppermute | solution.py:17
  125.6 26.2 %collective-permute-start.11 = (bf16[1,8,128,256]{3,2,1,0:T(8,128)(2,1)}, bf16[1,8,128,256]{3,2,1,0:T(8,128)(2,1)S(1)}, u32[]{:S(2)}, u32[]{:S(2)}) collective-permute-start(bf16[1,8,128,256]{3,2,1,0:T(8,128)(2,1)} %get-tuple-element.47), channel_id=1, source_target_pairs={{0,2},{2,4},{4,6},{6,8},{8,10},{10,12},{12,14},{1,3},{3,5},{5,7},{... | collective-permute-start | bytes 1572872 | tf_op jit(solution)/shard_map/ppermute | solution.py:15
  133.4 115.5 %reduce-scatter.3.cloned.1.call-start = ((), (), s32[]{:S(2)}) async-start(), calls=%async_computation.2 | async-start | bytes 278528 | tf_op jit(solution)/shard_map/reduce_scatter | solution.py:110
  133.4 18.4 %copy-start.5 = (bf16[4,8,128,256]{3,2,1,0:T(8,128)(2,1)S(1)}, bf16[4,8,128,256]{3,2,1,0:T(8,128)(2,1)}, u32[]{:S(2)}) copy-start(bf16[4,8,128,256]{3,2,1,0:T(8,128)(2,1)} %copy-done.4) | copy-start | bytes 6291460
  138.7 18.0 %copy-start.12 = (bf16[32,128,128]{2,1,0:T(8,128)(2,1)S(1)}, bf16[32,128,128]{2,1,0:T(8,128)(2,1)}, u32[]{:S(2)}) copy-start(bf16[32,128,128]{2,1,0:T(8,128)(2,1)} %gather_fusion.1) | copy-start | bytes 3145732
  138.7 18.0 %copy-start.26 = (pred[4,8]{1,0:T(4,128)(4,1)S(1)}, pred[4,8]{1,0:T(4,128)(4,1)}, u32[]{:S(2)}) copy-start(pred[4,8]{1,0:T(4,128)(4,1)} %copy-done.25) | copy-start | bytes 100
  151.9 10.3 %collective-permute-start.12 = (bf16[6,1,128,256]{3,2,1,0:T(8,128)(2,1)S(1)}, bf16[6,1,128,256]{3,2,1,0:T(8,128)(2,1)S(1)}, u32[]{:S(2)}, u32[]{:S(2)}) collective-permute-start(bf16[6,1,128,256]{3,2,1,0:T(8,128)(2,1)S(1)} %get-tuple-element.42), channel_id=1, source_target_pairs={{1,0},{3,2},{5,4},{7,6},{9,8},{11,10},{13,12},{15,14},{17,16},{19,... | collective-permute-start | bytes 1179656 | tf_op jit(solution)/shard_map/ppermute | solution.py:17
  153.2 6.2 %copy-start.10 = (bf16[4,8,128,128]{2,3,1,0:T(8,128)(2,1)S(1)}, bf16[4,8,128,128]{2,3,1,0:T(8,128)(2,1)}, u32[]{:S(2)}) copy-start(bf16[4,8,128,128]{2,3,1,0:T(8,128)(2,1)} %copy.15) | copy-start | bytes 3145732
  153.2 6.2 %copy-start.24 = (pred[4,8]{1,0:T(4,128)(4,1)S(1)}, pred[4,8]{1,0:T(4,128)(4,1)}, u32[]{:S(2)}) copy-start(pred[4,8]{1,0:T(4,128)(4,1)} %copy-done.23) | copy-start | bytes 100
  153.2 11.9 %collective-permute-start.13 = (bf16[6,1,128,256]{3,2,1,0:T(8,128)(2,1)S(1)}, bf16[6,1,128,256]{3,2,1,0:T(8,128)(2,1)S(1)}, u32[]{:S(2)}, u32[]{:S(2)}) collective-permute-start(bf16[6,1,128,256]{3,2,1,0:T(8,128)(2,1)S(1)} %get-tuple-element.41), channel_id=1, source_target_pairs={{0,1},{2,3},{4,5},{6,7},{8,9},{10,11},{12,13},{14,15},{16,17},{18,... | collective-permute-start | bytes 1179656 | tf_op jit(solution)/shard_map/ppermute | solution.py:15
  159.5 2.8 %copy-start.18 = (bf16[32,128,128]{2,1,0:T(8,128)(2,1)S(1)}, bf16[32,128,128]{2,1,0:T(8,128)(2,1)}, u32[]{:S(2)}) copy-start(bf16[32,128,128]{2,1,0:T(8,128)(2,1)} %gather_fusion.3) | copy-start | bytes 3145732
  159.5 2.8 %copy-start.30 = (pred[4,8]{1,0:T(4,128)(4,1)S(1)}, pred[4,8]{1,0:T(4,128)(4,1)}, u32[]{:S(2)}) copy-start(pred[4,8]{1,0:T(4,128)(4,1)} %copy-done.29) | copy-start | bytes 100
  178.5 70.4 %copy-start.1 = (bf16[16,128,128]{2,1,0:T(8,128)(2,1)S(1)}, bf16[16,128,128]{2,1,0:T(8,128)(2,1)}, u32[]{:S(2)}) copy-start(bf16[16,128,128]{2,1,0:T(8,128)(2,1)} %param.17) | copy-start | bytes 1572868
  (4 other events, 4.0 us)
Sparse Core Ops, SparseCore 0:
  133.5 56.8 reduce-scatter.4
  194.5 54.3 reduce-scatter.2
where the time goes:
time: 257 us; the launch traced here: 256 us
  matrix products  78 us (30%)
  waiting for transfers between devices  65.9 us (26%)
  starting transfers between devices  37.9 us (15%)
  blocking collectives  31.6 us (12%)
  local copies, waits for them, and re-layouts  26.4 us (10%)
  between operations  14.6 us (6%)
    reduce_scatter x1, waiting for transfers between devices, per_device(): lax.psum_scatter(column_term(m_one_flat, gz_one_flat), ('wide', 'narrow')...  35.9 us
    psum x1, blocking collectives, per_device(): grad_readout = lax.psum(local_readout, ('wide', 'narrow'))  31.6 us
    ppermute x6, starting transfers between devices, extended(): lax.ppermute(tail, axis, [(i, (i + 1) % count) for i in range(ends)])  23.5 us
    ppermute x6, waiting for transfers between devices, extended(): lax.ppermute(tail, axis, [(i, (i + 1) % count) for i in range(ends)])  22.9 us
    dot_general x2, matrix products, column_term(): lax.dot_general(matrix, grads, (((0,), (0,)), ((), ())), preferred_elemen...  15.6 us
    dot_general x3, matrix products, apply_operator(): jnp.einsum('xynm,xymh->xynh', selfs, centre, preferred_element_type=jnp.f...  12.9 us
    dot_general x2, matrix products, apply_operator(): jnp.einsum('xymn,xymh->xynh', south, padded[1:-1, :-2], preferred_element...  12 us
    dot_general x3, matrix products, apply_operator(): jnp.einsum('xynm,xymh->xynh', north, padded[1:-1, 2:], preferred_element_...  8.55 us
  transfers between devices with their start and end apart: 16, of which 5 were waited for; matrix products, arithmetic and copies ran while one was open for 30% of the time, Pallas kernels for 0%

commit v1 on v0

--- a/solution.py
+++ b/solution.py
@@ -89,7 +89,7 @@
     scale = jnp.sqrt(jnp.float32(width) / jnp.float32(nodes))
     grad_pred = (pred - target) * scale
     local_readout = jnp.einsum("xynh,xyn->h", x_two.astype(jnp.float32), grad_pred)
-    grad_readout = lax.psum(local_readout, ("wide", "narrow"))
+    grad_readout = jnp.sum(lax.all_gather(local_readout, ("wide", "narrow")), axis=0)
     grad_x_two = grad_pred[..., None] * readf
     tanh_two = jnp.tanh(z_two)
     grad_z_two = (grad_x_two * (1.0 - tanh_two * tanh_two)).astype(jnp.bfloat16)

time: 257 us -> 257 us (level)
  blocking collectives: 31.6 us -> 19.7 us
  waiting for transfers between devices: 65.9 us -> 77.3 us
    psum x1 -> x0, blocking collectives: 31.6 us -> none  [per_device(): grad_readout = lax.psum(local_readout, ('wide', 'narrow'))]
    all_gather x0 -> x1, blocking collectives: none -> 19.7 us  [per_device(): lax.all_gather(local_readout, ('wide', 'narrow'))]
    reduce_scatter x1, waiting for transfers between devices: 35.9 us -> 47.2 us  [per_device(): lax.psum_scatter(column_term(m_one_flat, gz_one_flat), ('wide', 'narrow')...]
where the time goes in v1:
time: 257 us; the launch traced here: 256 us
  matrix products  78 us (30%)
  waiting for transfers between devices  77.3 us (30%)
  starting transfers between devices  37.8 us (15%)
  local copies, waits for them, and re-layouts  26.3 us (10%)
  blocking collectives  19.7 us (8%)
  between operations  14.6 us (6%)
    reduce_scatter x1, waiting for transfers between devices, per_device(): lax.psum_scatter(column_term(m_one_flat, gz_one_flat), ('wide', 'narrow')...  47.2 us
    ppermute x6, starting transfers between devices, extended(): lax.ppermute(tail, axis, [(i, (i + 1) % count) for i in range(ends)])  23.5 us
    ppermute x6, waiting for transfers between devices, extended(): lax.ppermute(tail, axis, [(i, (i + 1) % count) for i in range(ends)])  22.9 us
    all_gather x1, blocking collectives, per_device(): lax.all_gather(local_readout, ('wide', 'narrow'))  19.7 us
    dot_general x2, matrix products, column_term(): lax.dot_general(matrix, grads, (((0,), (0,)), ((), ())), preferred_elemen...  15.6 us
    dot_general x3, matrix products, apply_operator(): jnp.einsum('xynm,xymh->xynh', selfs, centre, preferred_element_type=jnp.f...  12.8 us
    dot_general x2, matrix products, apply_operator(): jnp.einsum('xymn,xymh->xynh', south, padded[1:-1, :-2], preferred_element...  12 us
    dot_general x3, matrix products, apply_operator(): jnp.einsum('xynm,xymh->xynh', north, padded[1:-1, 2:], preferred_element_...  8.55 us
  transfers between devices with their start and end apart: 16, of which 5 were waited for; matrix products, arithmetic and copies ran while one was open for 30% of the time, Pallas kernels for 0%

profile of v1, /device:TPU:0, one launch (start us, length us, event | category | flops | bytes accessed | tf_op | source)
XLA Modules:
  0.0 255.8 jit_solution(6323042581942376033)
XLA Ops:
  8.0 4.9 %collective-permute-start = (s32[8]{0:T(128)S(1)}, s32[8]{0:T(128)S(1)}, u32[]{:S(2)}, u32[]{:S(2)}) collective-permute-start(s32[8]{0:T(128)S(1)} %slice_bitcast_fusion.5), channel_id=1, source_target_pairs={{0,2},{2,4},{4,6},{6,8},{8,10},{10,12},{12,14},{1,3},{3,5},{5,7},{... | collective-permute-start | bytes 104 | tf_op jit(solution)/shard_map/ppermute | solution.py:27
  13.7 1.5 collective-permute-start.1
  15.2 2.3 fusion.93
  17.5 3.4 %collective-permute-start.3 = (bf16[1,8,128,256]{3,2,1,0:T(8,128)(2,1)}, bf16[1,8,128,256]{3,2,1,0:T(8,128)(2,1)S(1)}, u32[]{:S(2)}, u32[]{:S(2)}) collective-permute-start(bf16[1,8,128,256]{3,2,1,0:T(8,128)(2,1)} %get-tuple-element.52), channel_id=1, source_target_pairs={{0,2},{2,4},{4,6},{6,8},{8,10},{10,12},{12,14},{1,3},{3,5},{5,7},{... | collective-permute-start | bytes 1572872 | tf_op jit(solution)/shard_map/ppermute | solution.py:15
  20.9 1.3 collective-permute-start.2
  24.9 1.7 gather_fusion
  26.5 2.3 copy.22
  28.8 4.0 %fusion.46 = f32[4,8,128,256]{3,2,1,0:T(8,128)} fusion(bf16[4,8,128,256]{3,2,1,0:T(8,128)(2,1)S(1)} %copy-done.2, bf16[4,8,128,128]{2,3,1,0:T(8,128)(2,1)} %copy.22, pred[4,8]{1,0:T(4,128)(4,1)S(1)} %get-tuple-element.57), kind=kOutput, calls=%fused_computation.84 | convolution fusion | flops 268959744 | bytes 7340064 | tf_op jit(solution)/shard_map/xymn,xymh->xynh/dot_general | solution.py:39
  32.8 1.6 gather_fusion.3
  34.6 1.7 gather_fusion.2
  36.3 2.3 copy.24
  38.5 1.7 gather_fusion.1
  40.2 1.7 gather_fusion.4
  41.9 2.3 copy.25
  44.2 4.4 %fusion.47 = f32[4,8,128,256]{3,2,1,0:T(8,128)} fusion(bf16[4,8,128,256]{3,2,1,0:T(8,128)(2,1)S(1)} %copy-done.2, bf16[4,8,128,128]{2,3,1,0:T(8,128)(2,1)} %copy.22, pred[4,8]{1,0:T(4,128)(4,1)S(1)} %get-tuple-element.57), kind=kOutput, calls=%fused_computation.85 | convolution fusion | flops 268959744 | bytes 7340064 | tf_op jit(solution)/shard_map/xynm,xymh->xynh/dot_general | solution.py:38
  50.0 1.3 collective-permute-start.4
  51.3 3.1 %collective-permute-start.5 = (bf16[6,1,128,256]{3,2,1,0:T(8,128)(2,1)S(1)}, bf16[6,1,128,256]{3,2,1,0:T(8,128)(2,1)S(1)}, u32[]{:S(2)}, u32[]{:S(2)}) collective-permute-start(bf16[6,1,128,256]{3,2,1,0:T(8,128)(2,1)S(1)} %get-tuple-element.45), channel_id=1, source_target_pairs={{0,1},{2,3},{4,5},{6,7},{8,9},{10,11},{12,13},{14,15},{16,17},{18,... | collective-permute-start | bytes 1179656 | tf_op jit(solution)/shard_map/ppermute | solution.py:15
  55.6 1.9 fusion.25
  57.6 2.9 %fusion.21 = f32[4,8,128,256]{3,2,1,0:T(8,128)} fusion(bf16[6,1,128,256]{3,2,1,0:T(8,128)(2,1)S(1)} %collective-permute-done.4, bf16[6,8,128,256]{3,2,1,0:T(8,128)(2,1)S(1)} %constant_dynamic-update-slice_fusion, bf16[4,8,128,128]{3,2,1,0:T(8,128)(2,1)S(1)} %bitcast.91, pred[4,8]{1,0:T(4,128)(4,1)S(1)} %get-tuple-element.54), kind=kOutput, calls=%fused_computation.50 | convolution fusion | flops 270008320 | bytes 8781856 | tf_op jit(solution)/shard_map/xynm,xymh->xynh/dot_general | solution.py:49
  61.5 7.3 %add_convert_fusion.3 = bf16[4,8,128,256]{3,2,1,0:T(8,128)(2,1)} fusion(f32[4,8,128,256]{3,2,1,0:T(8,128)} %fusion.21, f32[4,8,128,256]{3,2,1,0:T(8,128)S(1)} %fusion.23, f32[4,8,128,256]{3,2,1,0:T(8,128)S(1)} %fusion.25, f32[4,8,128,256]{3,2,1,0:T(8,128)} %fusion.47, f32[4,8,128,256]{3,2,1,0:T(8,128)S(1)} %copy-done.13, ...), kind=kOutput, calls=%fused_computation.13 | convolution fusion | flops 276299776 | bytes 27656224 | tf_op jit(solution)/shard_map/xymn,xymh->xynh/dot_general | solution.py:53
  68.8 4.3 %add_convert_fusion.2 = (bf16[4,8,128,256]{3,2,1,0:T(8,128)(2,1)S(1)}, f32[4,8,128,256]{3,2,1,0:T(8,128)}) fusion(bf16[4,8,128,256]{3,2,1,0:T(8,128)(2,1)S(1)} %copy-done.3, bf16[4,8,128,256]{3,2,1,0:T(8,128)(2,1)} %add_convert_fusion.3, bf16[256,256]{1,0:T(8,128)(2,1)S(1)} %copy-done.20), kind=kOutput, calls=%fused_computation.12 | convolution fusion | flops 540016640 | bytes 10616832 | tf_op jit(solution)/shard_map/xynh,hk->xynk/dot_general | solution.py:81
  73.3 1.4 collective-permute-start.6
  74.7 5.2 %collective-permute-start.7 = (bf16[1,8,128,256]{3,2,1,0:T(8,128)(2,1)S(1)}, bf16[1,8,128,256]{3,2,1,0:T(8,128)(2,1)S(1)}, u32[]{:S(2)}, u32[]{:S(2)}) collective-permute-start(bf16[1,8,128,256]{3,2,1,0:T(8,128)(2,1)S(1)} %get-tuple-element.49), channel_id=1, source_target_pairs={{0,2},{2,4},{4,6},{6,8},{8,10},{10,12},{12,14},{1,3},{3,5},{5,7},{... | collective-permute-start | bytes 1572872 | tf_op jit(solution)/shard_map/ppermute | solution.py:15
  80.7 3.2 %fusion.45 = f32[4,8,128,256]{3,2,1,0:T(8,128)} fusion(bf16[4,8,128,256]{3,2,1,0:T(8,128)(2,1)S(1)} %get-tuple-element.63, bf16[4,8,128,128]{2,3,1,0:T(8,128)(2,1)S(1)} %copy-done.6, pred[4,8]{1,0:T(4,128)(4,1)S(1)} %get-tuple-element.57), kind=kOutput, calls=%fused_computation.83 | convolution fusion | flops 268959744 | bytes 7340064 | tf_op jit(solution)/shard_map/xynm,xymh->xynh/dot_general | solution.py:38
  83.9 5.5 %collective-permute-done.6 = bf16[1,8,128,256]{3,2,1,0:T(8,128)(2,1)S(1)} collective-permute-done((bf16[1,8,128,256]{3,2,1,0:T(8,128)(2,1)S(1)}, bf16[1,8,128,256]{3,2,1,0:T(8,128)(2,1)S(1)}, u32[]{:S(2)}, u32[]{:S(2)}) %collective-permute-start.6) | collective-permute-done | bytes 524320 | tf_op jit(solution)/shard_map/ppermute | solution.py:17
  89.4 11.4 %collective-permute-done.7 = bf16[1,8,128,256]{3,2,1,0:T(8,128)(2,1)S(1)} collective-permute-done((bf16[1,8,128,256]{3,2,1,0:T(8,128)(2,1)S(1)}, bf16[1,8,128,256]{3,2,1,0:T(8,128)(2,1)S(1)}, u32[]{:S(2)}, u32[]{:S(2)}) %collective-permute-start.7) | collective-permute-done | bytes 524320 | tf_op jit(solution)/shard_map/ppermute | solution.py:15
  100.9 1.3 collective-permute-start.8
  102.2 3.3 %collective-permute-start.9 = (bf16[6,1,128,256]{3,2,1,0:T(8,128)(2,1)S(1)}, bf16[6,1,128,256]{3,2,1,0:T(8,128)(2,1)S(1)}, u32[]{:S(2)}, u32[]{:S(2)}) collective-permute-start(bf16[6,1,128,256]{3,2,1,0:T(8,128)(2,1)S(1)} %get-tuple-element.43), channel_id=1, source_target_pairs={{0,1},{2,3},{4,5},{6,7},{8,9},{10,11},{12,13},{14,15},{16,17},{18,... | collective-permute-start | bytes 1179656 | tf_op jit(solution)/shard_map/ppermute | solution.py:15
  107.5 2.8 %fusion.13 = f32[4,8,128,256]{3,2,1,0:T(8,128)} fusion(bf16[6,1,128,256]{3,2,1,0:T(8,128)(2,1)S(1)} %collective-permute-done.8, bf16[1,8,128,256]{3,2,1,0:T(8,128)(2,1)S(1)} %collective-permute-done.6, bf16[4,8,128,256]{3,2,1,0:T(8,128)(2,1)S(1)} %get-tuple-element.63, bf16[1,8,128,256]{3,2,1,0:T(8,128)(2,1)S(1)} %collective-permute-done.7, ...), kind=kOutput, calls=%fused_computation.36 | convolution fusion | flops 272105472 | bytes 8781856 | tf_op jit(solution)/shard_map/xynm,xymh->xynh/dot_general | solution.py:49
  110.2 4.7 %add_convert_fusion.1 = bf16[4,8,128,256]{3,2,1,0:T(8,128)(2,1)S(1)} fusion(f32[4,8,128,256]{3,2,1,0:T(8,128)} %fusion.13, f32[4,8,128,256]{3,2,1,0:T(8,128)S(1)} %fusion.15, f32[4,8,128,256]{3,2,1,0:T(8,128)S(1)} %fusion.17, f32[4,8,128,256]{3,2,1,0:T(8,128)} %fusion.45, f32[4,8,128,256]{3,2,1,0:T(8,128)S(1)} %fusion.44, ...), kind=kOutput, calls=%fused_computation.11 | convolution fusion | flops 278396928 | bytes 27656224 | tf_op jit(solution)/shard_map/xymn,xymh->xynh/dot_general | solution.py:53
  116.5 1.2 copy-done.8
  117.7 2.3 convolution_bitcast_fusion
  119.9 3.2 %convolution_convert_fusion = bf16[4,8,128,256]{3,2,1,0:T(8,128)(2,1)S(1)} fusion(bf16[256,256]{1,0:T(8,128)(2,1)S(1)} %copy-done.21, f32[4,8,128,256]{3,2,1,0:T(8,128)} %copy-done.8, f32[256]{0:T(256)S(1)} %copy-done.34, f32[4,8,128]{2,1,0:T(8,128)S(1)} %subtract_multiply_fusion), kind=kOutput, calls=%fused_computation.58 | convolution fusion | flops 543162368 | bytes 6439936 | tf_op jit(solution)/shard_map/xynk,hk->xynh/dot_general | solution.py:102
  124.2 1.4 collective-permute-start.10
  125.6 5.0 %collective-permute-start.11 = (bf16[1,8,128,256]{3,2,1,0:T(8,128)(2,1)}, bf16[1,8,128,256]{3,2,1,0:T(8,128)(2,1)S(1)}, u32[]{:S(2)}, u32[]{:S(2)}) collective-permute-start(bf16[1,8,128,256]{3,2,1,0:T(8,128)(2,1)} %get-tuple-element.47), channel_id=1, source_target_pairs={{0,2},{2,4},{4,6},{6,8},{8,10},{10,12},{12,14},{1,3},{3,5},{5,7},{... | collective-permute-start | bytes 1572872 | tf_op jit(solution)/shard_map/ppermute | solution.py:15
  130.7 2.7 %fusion.42 = f32[4,8,128,256]{3,2,1,0:T(8,128)} fusion(bf16[4,8,128,256]{3,2,1,0:T(8,128)(2,1)S(1)} %convolution_convert_fusion, bf16[4,8,128,128]{2,3,1,0:T(8,128)(2,1)S(1)} %copy-done.7, pred[4,8]{1,0:T(4,128)(4,1)S(1)} %copy-done.23), kind=kOutput, calls=%fused_computation.80 | convolution fusion | flops 268959744 | bytes 7340064 | tf_op jit(solution)/shard_map/xymn,xymh->xynh/dot_general | solution.py:39
  133.5 5.3 %fusion.43 = f32[4,8,128,256]{3,2,1,0:T(8,128)} fusion(bf16[4,8,128,256]{3,2,1,0:T(8,128)(2,1)} %copy-done.4, bf16[4,8,128,128]{2,3,1,0:T(8,128)(2,1)} %copy.22, pred[4,8]{1,0:T(4,128)(4,1)S(1)} %copy-done.23), kind=kOutput, calls=%fused_computation.81 | convolution fusion | flops 268959744 | bytes 7340064 | tf_op jit(solution)/shard_map/xynm,xymh->xynh/dot_general | solution.py:38
  138.8 1.6 collective-permute-done.10
  140.4 11.5 %collective-permute-done.11 = bf16[1,8,128,256]{3,2,1,0:T(8,128)(2,1)S(1)} collective-permute-done((bf16[1,8,128,256]{3,2,1,0:T(8,128)(2,1)}, bf16[1,8,128,256]{3,2,1,0:T(8,128)(2,1)S(1)}, u32[]{:S(2)}, u32[]{:S(2)}) %collective-permute-start.11) | collective-permute-done | bytes 524320 | tf_op jit(solution)/shard_map/ppermute | solution.py:15
  152.0 1.3 collective-permute-start.12
  153.3 3.4 %collective-permute-start.13 = (bf16[6,1,128,256]{3,2,1,0:T(8,128)(2,1)S(1)}, bf16[6,1,128,256]{3,2,1,0:T(8,128)(2,1)S(1)}, u32[]{:S(2)}, u32[]{:S(2)}) collective-permute-start(bf16[6,1,128,256]{3,2,1,0:T(8,128)(2,1)S(1)} %get-tuple-element.41), channel_id=1, source_target_pairs={{0,1},{2,3},{4,5},{6,7},{8,9},{10,11},{12,13},{14,15},{16,17},{18,... | collective-permute-start | bytes 1179656 | tf_op jit(solution)/shard_map/ppermute | solution.py:15
  156.8 2.8 %fusion.9 = f32[4,8,128,256]{3,2,1,0:T(8,128)} fusion(bf16[1,8,128,256]{3,2,1,0:T(8,128)(2,1)S(1)} %collective-permute-done.10, bf16[4,8,128,256]{3,2,1,0:T(8,128)(2,1)S(1)} %copy-done.5, bf16[4,8,128,128]{3,2,1,0:T(8,128)(2,1)S(1)} %bitcast.90, pred[4,8]{1,0:T(4,128)(4,1)S(1)} %copy-done.27), kind=kOutput, calls=%fused_computation.28 | convolution fusion | flops 270008320 | bytes 7864352 | tf_op jit(solution)/shard_map/xynm,xymh->xynh/dot_general | solution.py:41
  159.5 2.8 %fusion.7 = f32[4,8,128,256]{3,2,1,0:T(8,128)} fusion(bf16[4,8,128,256]{3,2,1,0:T(8,128)(2,1)S(1)} %copy-done.5, bf16[1,8,128,256]{3,2,1,0:T(8,128)(2,1)S(1)} %collective-permute-done.11, bf16[4,8,128,128]{2,3,1,0:T(8,128)(2,1)S(1)} %copy-done.10, pred[4,8]{1,0:T(4,128)(4,1)S(1)} %copy-done.25), kind=kOutput, calls=%fused_computation.25 | convolution fusion | flops 270008320 | bytes 7864352 | tf_op jit(solution)/shard_map/xymn,xymh->xynh/dot_general | solution.py:45
  162.3 2.9 %fusion.5 = f32[4,8,128,256]{3,2,1,0:T(8,128)} fusion(bf16[6,1,128,256]{3,2,1,0:T(8,128)(2,1)S(1)} %collective-permute-done.12, bf16[1,8,128,256]{3,2,1,0:T(8,128)(2,1)S(1)} %collective-permute-done.10, bf16[4,8,128,256]{3,2,1,0:T(8,128)(2,1)S(1)} %copy-done.5, bf16[1,8,128,256]{3,2,1,0:T(8,128)(2,1)S(1)} %collective-permute-done.11, ...), kind=kOutput, calls=%fused_computation.20 | convolution fusion | flops 272105472 | bytes 8781856 | tf_op jit(solution)/shard_map/xynm,xymh->xynh/dot_general | solution.py:49
  165.2 13.3 %fusion.28 = f32[256,256]{1,0:T(8,128)} fusion(bf16[4,8,128,256]{3,2,1,0:T(8,128)(2,1)} %add_convert_fusion.3, f32[4,8,128,256]{3,2,1,0:T(8,128)} %fusion.5, f32[4,8,128,256]{3,2,1,0:T(8,128)} %fusion.7, f32[4,8,128,256]{3,2,1,0:T(8,128)} %fusion.9, f32[4,8,128,256]{3,2,1,0:T(8,128)} %fusion.43, f32[4,8,128,256]{3,2,1,0:T(8,128)} %fusion.42, ...), kind=kOutput, calls=%fused_computation.60 | convolution fusion | flops 820510720 | bytes 32130080 | tf_op jit(solution)/shard_map/dot_general | solution.py:64
  178.5 2.9 %convolution_bitcast_fusion.1 = f32[1,1,256]{2,1,0:T(1,128)S(1)} fusion(f32[4,8,128,1]{2,3,1,0:T(1,128)S(1)} %bitcast.97, bf16[4,8,128,256]{3,2,1,0:T(8,128)(2,1)S(1)} %get-tuple-element.63, f32[4,8,128,256]{3,2,1,0:T(8,128)} %copy-done.8), kind=kOutput, calls=%fused_computation.62 | convolution fusion | flops 5242880 | bytes 6308864 | tf_op jit(solution)/shard_map/xynh,xyn->h/dot_general | solution.py:91
  181.4 19.7 %all-gather.1 = f32[16,1,256]{2,1,0:T(1,128)S(1)} all-gather(f32[1,1,256]{2,1,0:T(1,128)S(1)} %convolution_bitcast_fusion.1), channel_id=2, replica_groups=mesh['groups'=2,'wide'=8,'narrow'=2] {'wide','narrow'}, dimensions={0}, use_global_device_ids=true | all-gather | bytes 17408 | tf_op jit(solution)/shard_map/all_gather | solution.py:92
  201.7 47.2 %reduce-scatter.3.cloned.1.call-done = f32[16,256]{1,0:T(8,128)} async-done(((f32[256,256]{1,0:T(8,128)}), f32[16,256]{1,0:T(8,128)}) %reduce-scatter.3.cloned.1.call-update) | async-done | bytes 16400 | tf_op jit(solution)/shard_map/reduce_scatter | solution.py:110
  (122 shorter events, 14.4 us)
Async XLA Ops:
  7.2 17.7 %copy-start = (bf16[16,128,128]{2,1,0:T(8,128)(2,1)S(1)}, bf16[16,128,128]{2,1,0:T(8,128)(2,1)}, u32[]{:S(2)}) copy-start(bf16[16,128,128]{2,1,0:T(8,128)(2,1)} %param.17) | copy-start | bytes 1572868
  7.2 16.2 %copy-start.32 = (s32[4,8,3]{1,0,2:T(4,128)S(1)}, s32[4,8,3]{1,0,2:T(4,128)}, u32[]{:S(2)}) copy-start(s32[4,8,3]{1,0,2:T(4,128)} %param.16) | copy-start | bytes 1156
  7.2 15.0 %copy-start.36 = (bf16[256]{0:T(256)(128)(2,1)S(1)}, bf16[256]{0:T(256)(128)(2,1)}, u32[]{:S(2)}) copy-start(bf16[256]{0:T(256)(128)(2,1)} %param.20) | copy-start | bytes 1540
  7.2 194.5 %reduce-scatter.5.cloned.1.call-start = ((), (), s32[]{:S(2)}) async-start(), calls=%async_computation.3 | async-start | bytes 278528 | tf_op jit(solution)/shard_map/reduce_scatter | solution.py:99
  8.0 15.6 %collective-permute-start = (s32[8]{0:T(128)S(1)}, s32[8]{0:T(128)S(1)}, u32[]{:S(2)}, u32[]{:S(2)}) collective-permute-start(s32[8]{0:T(128)S(1)} %slice_bitcast_fusion.5), channel_id=1, source_target_pairs={{0,2},{2,4},{4,6},{6,8},{8,10},{10,12},{12,14},{1,3},{3,5},{5,7},{... | collective-permute-start | bytes 104 | tf_op jit(solution)/shard_map/ppermute | solution.py:27
  13.7 9.7 %collective-permute-start.1 = (s32[4]{0:T(128)S(1)}, s32[4]{0:T(128)S(1)}, u32[]{:S(2)}, u32[]{:S(2)}) collective-permute-start(s32[4]{0:T(128)S(1)} %slice_reduce_fusion), channel_id=1, source_target_pairs={{0,1},{2,3},{4,5},{6,7},{8,9},{10,11},{12,13},{14,15},{16,17},{18,... | collective-permute-start | bytes 56 | tf_op jit(solution)/shard_map/ppermute | solution.py:27
  17.5 31.1 %collective-permute-start.3 = (bf16[1,8,128,256]{3,2,1,0:T(8,128)(2,1)}, bf16[1,8,128,256]{3,2,1,0:T(8,128)(2,1)S(1)}, u32[]{:S(2)}, u32[]{:S(2)}) collective-permute-start(bf16[1,8,128,256]{3,2,1,0:T(8,128)(2,1)} %get-tuple-element.52), channel_id=1, source_target_pairs={{0,2},{2,4},{4,6},{6,8},{8,10},{10,12},{12,14},{1,3},{3,5},{5,7},{... | collective-permute-start | bytes 1572872 | tf_op jit(solution)/shard_map/ppermute | solution.py:15
  20.9 27.8 %collective-permute-start.2 = (bf16[1,8,128,256]{3,2,1,0:T(8,128)(2,1)}, bf16[1,8,128,256]{3,2,1,0:T(8,128)(2,1)}, u32[]{:S(2)}, u32[]{:S(2)}) collective-permute-start(bf16[1,8,128,256]{3,2,1,0:T(8,128)(2,1)} %get-tuple-element.51), channel_id=1, source_target_pairs={{2,0},{4,2},{6,4},{8,6},{10,8},{12,10},{14,12},{3,1},{5,3},{7,5},{... | collective-permute-start | bytes 1572872 | tf_op jit(solution)/shard_map/ppermute | solution.py:17
  24.6 56.1 %copy-start.22 = (pred[4,8]{1,0:T(4,128)(4,1)}, pred[4,8]{1,0:T(4,128)(4,1)S(1)}, u32[]{:S(2)}) copy-start(pred[4,8]{1,0:T(4,128)(4,1)S(1)} %get-tuple-element.57) | copy-start | bytes 100
  24.6 80.9 %copy-start.26 = (pred[4,8]{1,0:T(4,128)(4,1)}, pred[4,8]{1,0:T(4,128)(4,1)S(1)}, u32[]{:S(2)}) copy-start(pred[4,8]{1,0:T(4,128)(4,1)S(1)} %get-tuple-element.56) | copy-start | bytes 100
  24.6 81.6 %copy-start.24 = (pred[4,8]{1,0:T(4,128)(4,1)}, pred[4,8]{1,0:T(4,128)(4,1)S(1)}, u32[]{:S(2)}) copy-start(pred[4,8]{1,0:T(4,128)(4,1)S(1)} %get-tuple-element.55) | copy-start | bytes 100
  24.6 82.5 %copy-start.30 = (pred[4,8]{1,0:T(4,128)(4,1)}, pred[4,8]{1,0:T(4,128)(4,1)S(1)}, u32[]{:S(2)}) copy-start(pred[4,8]{1,0:T(4,128)(4,1)S(1)} %get-tuple-element.54) | copy-start | bytes 100
  24.8 4.0 %copy-start.2 = (bf16[4,8,128,256]{3,2,1,0:T(8,128)(2,1)S(1)}, bf16[4,8,128,256]{3,2,1,0:T(8,128)(2,1)}, u32[]{:S(2)}) copy-start(bf16[4,8,128,256]{3,2,1,0:T(8,128)(2,1)} %param.15) | copy-start | bytes 6291460
  48.7 5.6 %copy-start.9 = (bf16[4,8,128,128]{2,3,1,0:T(8,128)(2,1)S(1)}, bf16[4,8,128,128]{2,3,1,0:T(8,128)(2,1)}, u32[]{:S(2)}) copy-start(bf16[4,8,128,128]{2,3,1,0:T(8,128)(2,1)} %copy.24) | copy-start | bytes 3145732
  49.9 7.6 %copy-start.14 = (bf16[6,8,128,256]{3,2,1,0:T(8,128)(2,1)}, bf16[6,8,128,256]{3,2,1,0:T(8,128)(2,1)S(1)}, u32[]{:S(2)}) copy-start(bf16[6,8,128,256]{3,2,1,0:T(8,128)(2,1)S(1)} %constant_dynamic-update-slice_fusion) | copy-start | bytes 9437188
  50.0 7.5 %collective-permute-start.4 = (bf16[6,1,128,256]{3,2,1,0:T(8,128)(2,1)S(1)}, bf16[6,1,128,256]{3,2,1,0:T(8,128)(2,1)S(1)}, u32[]{:S(2)}, u32[]{:S(2)}) collective-permute-start(bf16[6,1,128,256]{3,2,1,0:T(8,128)(2,1)S(1)} %get-tuple-element.46), channel_id=1, source_target_pairs={{1,0},{3,2},{5,4},{7,6},{9,8},{11,10},{13,12},{15,14},{17,16},{19,... | collective-permute-start | bytes 1179656 | tf_op jit(solution)/shard_map/ppermute | solution.py:17
  51.3 9.2 %collective-permute-start.5 = (bf16[6,1,128,256]{3,2,1,0:T(8,128)(2,1)S(1)}, bf16[6,1,128,256]{3,2,1,0:T(8,128)(2,1)S(1)}, u32[]{:S(2)}, u32[]{:S(2)}) collective-permute-start(bf16[6,1,128,256]{3,2,1,0:T(8,128)(2,1)S(1)} %get-tuple-element.45), channel_id=1, source_target_pairs={{0,1},{2,3},{4,5},{6,7},{8,9},{10,11},{12,13},{14,15},{16,17},{18,... | collective-permute-start | bytes 1179656 | tf_op jit(solution)/shard_map/ppermute | solution.py:15
  57.5 3.3 %copy-start.13 = (f32[4,8,128,256]{3,2,1,0:T(8,128)S(1)}, f32[4,8,128,256]{3,2,1,0:T(8,128)}, u32[]{:S(2)}) copy-start(f32[4,8,128,256]{3,2,1,0:T(8,128)} %fusion.46) | copy-start | bytes 12582916
  57.5 4.0 %copy-start.15 = (bf16[4,8,128,128]{2,3,1,0:T(8,128)(2,1)S(1)}, bf16[4,8,128,128]{2,3,1,0:T(8,128)(2,1)}, u32[]{:S(2)}) copy-start(bf16[4,8,128,128]{2,3,1,0:T(8,128)(2,1)} %copy.25) | copy-start | bytes 3145732
  57.6 4.0 %copy-start.33 = (pred[4,8]{1,0:T(4,128)(4,1)S(1)}, pred[4,8]{1,0:T(4,128)(4,1)}, u32[]{:S(2)}) copy-start(pred[4,8]{1,0:T(4,128)(4,1)} %get-tuple-element.53) | copy-start | bytes 100
  61.5 7.3 %copy-start.3 = (bf16[4,8,128,256]{3,2,1,0:T(8,128)(2,1)S(1)}, bf16[4,8,128,256]{3,2,1,0:T(8,128)(2,1)}, u32[]{:S(2)}) copy-start(bf16[4,8,128,256]{3,2,1,0:T(8,128)(2,1)} %param.15) | copy-start | bytes 6291460
  61.5 7.3 %copy-start.20 = (bf16[256,256]{1,0:T(8,128)(2,1)S(1)}, bf16[256,256]{1,0:T(8,128)(2,1)}, u32[]{:S(2)}) copy-start(bf16[256,256]{1,0:T(8,128)(2,1)} %param.18) | copy-start | bytes 393220
  73.2 6.7 %copy-start.6 = (bf16[4,8,128,128]{2,3,1,0:T(8,128)(2,1)S(1)}, bf16[4,8,128,128]{2,3,1,0:T(8,128)(2,1)}, u32[]{:S(2)}) copy-start(bf16[4,8,128,128]{2,3,1,0:T(8,128)(2,1)} %copy.22) | copy-start | bytes 3145732
  73.3 16.1 %collective-permute-start.6 = (bf16[1,8,128,256]{3,2,1,0:T(8,128)(2,1)S(1)}, bf16[1,8,128,256]{3,2,1,0:T(8,128)(2,1)S(1)}, u32[]{:S(2)}, u32[]{:S(2)}) collective-permute-start(bf16[1,8,128,256]{3,2,1,0:T(8,128)(2,1)S(1)} %get-tuple-element.50), channel_id=1, source_target_pairs={{2,0},{4,2},{6,4},{8,6},{10,8},{12,10},{14,12},{3,1},{5,3},{7,5},{... | collective-permute-start | bytes 1572872 | tf_op jit(solution)/shard_map/ppermute | solution.py:17
  74.7 26.1 %collective-permute-start.7 = (bf16[1,8,128,256]{3,2,1,0:T(8,128)(2,1)S(1)}, bf16[1,8,128,256]{3,2,1,0:T(8,128)(2,1)S(1)}, u32[]{:S(2)}, u32[]{:S(2)}) collective-permute-start(bf16[1,8,128,256]{3,2,1,0:T(8,128)(2,1)S(1)} %get-tuple-element.49), channel_id=1, source_target_pairs={{0,2},{2,4},{4,6},{6,8},{8,10},{10,12},{12,14},{1,3},{3,5},{5,7},{... | collective-permute-start | bytes 1572872 | tf_op jit(solution)/shard_map/ppermute | solution.py:15
  100.9 6.2 %collective-permute-start.8 = (bf16[6,1,128,256]{3,2,1,0:T(8,128)(2,1)S(1)}, bf16[6,1,128,256]{3,2,1,0:T(8,128)(2,1)S(1)}, u32[]{:S(2)}, u32[]{:S(2)}) collective-permute-start(bf16[6,1,128,256]{3,2,1,0:T(8,128)(2,1)S(1)} %get-tuple-element.44), channel_id=1, source_target_pairs={{1,0},{3,2},{5,4},{7,6},{9,8},{11,10},{13,12},{15,14},{17,16},{19,... | collective-permute-start | bytes 1179656 | tf_op jit(solution)/shard_map/ppermute | solution.py:17
  102.2 8.1 %collective-permute-start.9 = (bf16[6,1,128,256]{3,2,1,0:T(8,128)(2,1)S(1)}, bf16[6,1,128,256]{3,2,1,0:T(8,128)(2,1)S(1)}, u32[]{:S(2)}, u32[]{:S(2)}) collective-permute-start(bf16[6,1,128,256]{3,2,1,0:T(8,128)(2,1)S(1)} %get-tuple-element.43), channel_id=1, source_target_pairs={{0,1},{2,3},{4,5},{6,7},{8,9},{10,11},{12,13},{14,15},{16,17},{18,... | collective-permute-start | bytes 1179656 | tf_op jit(solution)/shard_map/ppermute | solution.py:15
  107.0 3.2 %copy-start.16 = (bf16[4,8,128,128]{2,3,1,0:T(8,128)(2,1)S(1)}, bf16[4,8,128,128]{2,3,1,0:T(8,128)(2,1)}, u32[]{:S(2)}) copy-start(bf16[4,8,128,128]{2,3,1,0:T(8,128)(2,1)} %copy.25) | copy-start | bytes 3145732
  110.2 4.7 %copy-start.21 = (bf16[256,256]{1,0:T(8,128)(2,1)S(1)}, bf16[256,256]{1,0:T(8,128)(2,1)}, u32[]{:S(2)}) copy-start(bf16[256,256]{1,0:T(8,128)(2,1)} %param.19) | copy-start | bytes 393220
  115.7 2.0 copy-start.8
  115.7 2.0 copy-start.34
  116.5 3.5 %copy-start.28 = (f32[1,4,8,128]{3,0,2,1:T(1,128)}, f32[1,4,8,128]{3,0,2,1:T(1,128)S(1)}, u32[]{:S(2)}) copy-start(f32[1,4,8,128]{3,0,2,1:T(1,128)S(1)} %fusion.53) | copy-start | bytes 49156
  123.1 7.6 %copy-start.4 = (bf16[4,8,128,256]{3,2,1,0:T(8,128)(2,1)}, bf16[4,8,128,256]{3,2,1,0:T(8,128)(2,1)S(1)}, u32[]{:S(2)}) copy-start(bf16[4,8,128,256]{3,2,1,0:T(8,128)(2,1)S(1)} %convolution_convert_fusion) | copy-start | bytes 6291460
  123.1 7.6 %copy-start.7 = (bf16[4,8,128,128]{2,3,1,0:T(8,128)(2,1)S(1)}, bf16[4,8,128,128]{2,3,1,0:T(8,128)(2,1)}, u32[]{:S(2)}) copy-start(bf16[4,8,128,128]{2,3,1,0:T(8,128)(2,1)} %copy.22) | copy-start | bytes 3145732
  123.1 7.6 %copy-start.23 = (pred[4,8]{1,0:T(4,128)(4,1)S(1)}, pred[4,8]{1,0:T(4,128)(4,1)}, u32[]{:S(2)}) copy-start(pred[4,8]{1,0:T(4,128)(4,1)} %copy-done.22) | copy-start | bytes 100
  124.2 16.2 %collective-permute-start.10 = (bf16[1,8,128,256]{3,2,1,0:T(8,128)(2,1)}, bf16[1,8,128,256]{3,2,1,0:T(8,128)(2,1)S(1)}, u32[]{:S(2)}, u32[]{:S(2)}) collective-permute-start(bf16[1,8,128,256]{3,2,1,0:T(8,128)(2,1)} %get-tuple-element.48), channel_id=1, source_target_pairs={{2,0},{4,2},{6,4},{8,6},{10,8},{12,10},{14,12},{3,1},{5,3},{7,5},{... | collective-permute-start | bytes 1572872 | tf_op jit(solution)/shard_map/ppermute | solution.py:17
  125.6 26.2 %collective-permute-start.11 = (bf16[1,8,128,256]{3,2,1,0:T(8,128)(2,1)}, bf16[1,8,128,256]{3,2,1,0:T(8,128)(2,1)S(1)}, u32[]{:S(2)}, u32[]{:S(2)}) collective-permute-start(bf16[1,8,128,256]{3,2,1,0:T(8,128)(2,1)} %get-tuple-element.47), channel_id=1, source_target_pairs={{0,2},{2,4},{4,6},{6,8},{8,10},{10,12},{12,14},{1,3},{3,5},{5,7},{... | collective-permute-start | bytes 1572872 | tf_op jit(solution)/shard_map/ppermute | solution.py:15
  133.4 115.5 %reduce-scatter.3.cloned.1.call-start = ((), (), s32[]{:S(2)}) async-start(), calls=%async_computation.2 | async-start | bytes 278528 | tf_op jit(solution)/shard_map/reduce_scatter | solution.py:110
  133.5 18.4 %copy-start.5 = (bf16[4,8,128,256]{3,2,1,0:T(8,128)(2,1)S(1)}, bf16[4,8,128,256]{3,2,1,0:T(8,128)(2,1)}, u32[]{:S(2)}) copy-start(bf16[4,8,128,256]{3,2,1,0:T(8,128)(2,1)} %copy-done.4) | copy-start | bytes 6291460
  138.8 18.0 %copy-start.12 = (bf16[32,128,128]{2,1,0:T(8,128)(2,1)S(1)}, bf16[32,128,128]{2,1,0:T(8,128)(2,1)}, u32[]{:S(2)}) copy-start(bf16[32,128,128]{2,1,0:T(8,128)(2,1)} %gather_fusion.1) | copy-start | bytes 3145732
  138.8 18.0 %copy-start.27 = (pred[4,8]{1,0:T(4,128)(4,1)S(1)}, pred[4,8]{1,0:T(4,128)(4,1)}, u32[]{:S(2)}) copy-start(pred[4,8]{1,0:T(4,128)(4,1)} %copy-done.26) | copy-start | bytes 100
  152.0 10.3 %collective-permute-start.12 = (bf16[6,1,128,256]{3,2,1,0:T(8,128)(2,1)S(1)}, bf16[6,1,128,256]{3,2,1,0:T(8,128)(2,1)S(1)}, u32[]{:S(2)}, u32[]{:S(2)}) collective-permute-start(bf16[6,1,128,256]{3,2,1,0:T(8,128)(2,1)S(1)} %get-tuple-element.42), channel_id=1, source_target_pairs={{1,0},{3,2},{5,4},{7,6},{9,8},{11,10},{13,12},{15,14},{17,16},{19,... | collective-permute-start | bytes 1179656 | tf_op jit(solution)/shard_map/ppermute | solution.py:17
  153.3 6.2 %copy-start.10 = (bf16[4,8,128,128]{2,3,1,0:T(8,128)(2,1)S(1)}, bf16[4,8,128,128]{2,3,1,0:T(8,128)(2,1)}, u32[]{:S(2)}) copy-start(bf16[4,8,128,128]{2,3,1,0:T(8,128)(2,1)} %copy.24) | copy-start | bytes 3145732
  153.3 6.2 %copy-start.25 = (pred[4,8]{1,0:T(4,128)(4,1)S(1)}, pred[4,8]{1,0:T(4,128)(4,1)}, u32[]{:S(2)}) copy-start(pred[4,8]{1,0:T(4,128)(4,1)} %copy-done.24) | copy-start | bytes 100
  153.3 11.9 %collective-permute-start.13 = (bf16[6,1,128,256]{3,2,1,0:T(8,128)(2,1)S(1)}, bf16[6,1,128,256]{3,2,1,0:T(8,128)(2,1)S(1)}, u32[]{:S(2)}, u32[]{:S(2)}) collective-permute-start(bf16[6,1,128,256]{3,2,1,0:T(8,128)(2,1)S(1)} %get-tuple-element.41), channel_id=1, source_target_pairs={{0,1},{2,3},{4,5},{6,7},{8,9},{10,11},{12,13},{14,15},{16,17},{18,... | collective-permute-start | bytes 1179656 | tf_op jit(solution)/shard_map/ppermute | solution.py:15
  159.5 2.8 %copy-start.19 = (bf16[32,128,128]{2,1,0:T(8,128)(2,1)S(1)}, bf16[32,128,128]{2,1,0:T(8,128)(2,1)}, u32[]{:S(2)}) copy-start(bf16[32,128,128]{2,1,0:T(8,128)(2,1)} %gather_fusion.3) | copy-start | bytes 3145732
  159.5 2.8 %copy-start.31 = (pred[4,8]{1,0:T(4,128)(4,1)S(1)}, pred[4,8]{1,0:T(4,128)(4,1)}, u32[]{:S(2)}) copy-start(pred[4,8]{1,0:T(4,128)(4,1)} %copy-done.30) | copy-start | bytes 100
  178.5 70.5 %copy-start.1 = (bf16[16,128,128]{2,1,0:T(8,128)(2,1)S(1)}, bf16[16,128,128]{2,1,0:T(8,128)(2,1)}, u32[]{:S(2)}) copy-start(bf16[16,128,128]{2,1,0:T(8,128)(2,1)} %param.17) | copy-start | bytes 1572868
  (5 other events, 5.9 us)
Sparse Core Ops, SparseCore 0:
  133.6 56.8 reduce-scatter.4
  194.6 54.3 reduce-scatter.2
